TPU v7x, 32 devices: a whole 2x2x4 slice. The times are simulated.
32 devices in a mesh: band: 4 (over y, x), patch: 8 (over z, core).
Axes of the slice: x: 2, y: 2, z: 4, core: 2. Of those that a mesh axis runs over, the one named last changes fastest.
Arguments:
- emissivity: float32 [32, 65536], P('band', 'patch'), may hold values from 0.1 to 0.9
- blackbody: float32 [32, 65536], P('band', 'patch'), may hold values from 0.2 to 2
- loss_weights: float32 [32, 65536], P('band', 'patch'), may hold values from 0.5 to 1.5
- view_blocks: bfloat16 [8, 4, 8, 16, 256, 256], P('patch', 'band'), may hold values from 0 to 0.012207031
- column_blocks: int32 [8, 4, 8, 16], P('patch', 'band'), may hold values from 0 to 255, as said below
- patch_owner: int32 [8, 4, 2048, 1], P('patch', 'band'), may hold values from 0 to 31; in each aligned block of 2048 rows (0 to 2047, 2048 to 4095, ..., all dimensions but the last counted through in order) at most 192 rows name the same one
- patch_surface: int32 [8, 4, 2048], P('patch', 'band'), may hold values from 0 to 1023
Outputs:
- radiosity: float32 [32, 8, 4, 2048], P(None, 'patch', 'band')
- surface_grad: float32 [32, 32768], P(None, ('band', 'patch'))
Inputs may be any that keep to these rules, and one draw needn't show every extreme that they name: column_blocks[g, s, r] lists 16 different row-block indices, all among the 96 row blocks of patch groups g - 1, g and g + 1, wrapping around the 8 groups. `patch_owner`: among the 2048 patches of one row-block range no owner is named more than 192 times.
All inputs are finite; a program needn't handle non-finite values.
Results may differ from a plain program's by a relative error of at most 0.0005.
Values may be sent and summed in bfloat16 or wider, within the bound.
No kernel may reach another device: no remote copies, remote signals or barrier semaphores. Data moves between devices by JAX's collectives and lax.ppermute only.
A program may use at most 128 MiB of HBM per device.

v0:
```python
import jax
import jax.numpy as jnp
from jax import lax
from jax.sharding import PartitionSpec as P


def passed_along(block, axis, distance):
    devices = range(lax.axis_size(axis))
    route = [((i - distance) % len(devices), i) for i in devices]
    return lax.ppermute(block, axis, route)


def body(
    emissivity, blackbody, loss_weights, view_blocks, column_blocks, patch_owner, patch_surface
):
    emissive, planck, weighting = (
        lax.all_to_all(emissivity, "band", split_axis=1, concat_axis=0, tiled=True),
        lax.all_to_all(blackbody, "band", split_axis=1, concat_axis=0, tiled=True),
        lax.all_to_all(loss_weights, "band", split_axis=1, concat_axis=0, tiled=True),
    )
    band_count = emissive.shape[0]
    patch_rows = emissive.shape[1]
    rb_count = view_blocks.shape[2]
    depth = view_blocks.shape[3]
    width = view_blocks.shape[4]
    split_count = lax.axis_size("band")
    group_count = lax.axis_size("patch")
    per_group = split_count * rb_count
    block_total = group_count * per_group
    window_start = (lax.axis_index("patch") - 1) * per_group
    offsets = jnp.mod(column_blocks.reshape(rb_count, depth) - window_start, block_total)
    flat_offsets = offsets.reshape(rb_count * depth)
    matrix = view_blocks.reshape(rb_count, depth, width, width)
    emission = emissive * planck
    reflect = 1.0 - emissive

    def window(vector):
        gathered = lax.all_gather(vector, "band", axis=1, tiled=True)
        lower_rows = passed_along(gathered, "patch", 1)
        upper_rows = passed_along(gathered, "patch", -1)
        joined = jnp.concatenate([lower_rows, gathered, upper_rows], axis=1)
        return joined.reshape(band_count, 3 * per_group, width)

    def forward(vector):
        blocks = window(vector)
        picked = blocks[:, offsets]
        result = jnp.einsum("rkij,brkj->bri", matrix, picked, preferred_element_type=jnp.float32)
        return result.reshape(band_count, patch_rows)

    def adjoint(vector):
        partial_terms = jnp.einsum(
            "rkij,bri->brkj",
            matrix,
            vector.reshape(band_count, rb_count, width),
            preferred_element_type=jnp.float32,
        )
        empty = jnp.zeros((band_count, 3 * per_group, width), jnp.float32)
        totals = empty.at[:, flat_offsets].add(
            partial_terms.reshape(band_count, rb_count * depth, width)
        )
        totals = totals.reshape(band_count, 3, split_count, patch_rows)
        from_upper = passed_along(totals[:, 0].astype(jnp.bfloat16), "patch", -1).astype(
            jnp.float32
        )
        from_lower = passed_along(totals[:, 2], "patch", 1)
        combined = totals[:, 1] + from_upper + from_lower
        return lax.psum_scatter(combined, "band", scatter_dimension=1, tiled=True).reshape(
            band_count, patch_rows
        )

    incident_zero = forward(emission.astype(jnp.bfloat16))
    rad_one = emission + reflect * incident_zero
    incident_one = forward(rad_one.astype(jnp.bfloat16))
    radiosity = emission + reflect * incident_one
    adjoint_one = adjoint((reflect * weighting).astype(jnp.bfloat16))
    adjoint_zero = adjoint((reflect * adjoint_one).astype(jnp.bfloat16))
    gradient = (weighting + adjoint_one + adjoint_zero) * planck - (
        weighting * incident_one + adjoint_one * incident_zero
    )
    device_count = split_count * group_count
    capacity = max(2, 3 * patch_rows // device_count)
    surface_count = patch_rows // 2
    owners = patch_owner.reshape(patch_rows)
    locals_index = patch_surface.reshape(patch_rows)
    owner_hits = (owners[:, None] == jnp.arange(device_count, dtype=jnp.int32)[None, :]).astype(
        jnp.int32
    )
    running = jnp.cumsum(owner_hits, axis=0)
    slot_index = jnp.sum(running * owner_hits, axis=1) - 1
    send_values = (
        jnp.zeros((band_count, device_count, capacity), jnp.float32)
        .at[:, owners, slot_index]
        .set(gradient)
    )
    send_labels = (
        jnp.full((1, device_count, capacity), surface_count, jnp.int32)
        .at[0, owners, slot_index]
        .set(locals_index)
    )
    got_values, got_labels = (
        lax.all_to_all(send_values, ("band", "patch"), split_axis=1, concat_axis=1, tiled=True),
        lax.all_to_all(send_labels, ("band", "patch"), split_axis=1, concat_axis=1, tiled=True),
    )
    flat_values = got_values.reshape(band_count, device_count * capacity)
    flat_labels = got_labels.reshape(device_count * capacity)
    surface_sums = jax.ops.segment_sum(flat_values.T, flat_labels, surface_count + 1)[
        :surface_count
    ].T
    surface_counts = jax.ops.segment_sum(
        jnp.ones((device_count * capacity,), jnp.float32), flat_labels, surface_count + 1
    )[:surface_count]
    surface_grad = surface_sums / jnp.maximum(surface_counts, 1.0)[None, :]
    return (radiosity.reshape(band_count, 1, 1, patch_rows), surface_grad)


def solution(mesh):
    in_specs = (
        P("band", "patch"),
        P("band", "patch"),
        P("band", "patch"),
        P("patch", "band", None, None, None, None),
        P("patch", "band", None, None),
        P("patch", "band", None, None),
        P("patch", "band", None),
    )
    out_specs = (P(None, "patch", "band", None), P(None, ("band", "patch")))
    return jax.shard_map(body, mesh=mesh, in_specs=in_specs, out_specs=out_specs, check_vma=False)
```

profile of v0, /device:TPU:1, one launch (start us, length us, event | category | flops | bytes accessed | tf_op | source)
XLA Modules:
  0.0 336.8 jit_solution(3225798159353689433)
XLA Ops:
  7.2 4.3 %all-to-all-start = ((f32[8,4,2048]{2,0,1:T(8,128)}), f32[8,4,2048]{2,0,1:T(8,128)S(1)}, u32[]{:S(2)}, u32[]{:S(2)}) async-start(f32[8,4,2048]{2,0,1:T(8,128)} %bitcast.215), calls=%async_computation | async-start | bytes 524288 | tf_op jit(solution)/shard_map/all_to_all | solution.py:17
  13.1 9.1 %reduce-window.6 = s32[32,16,128]{2,1,0:T(8,128)S(1)} reduce-window(s32[32,16,128]{2,1,0:T(8,128)S(1)} %fusion.35, s32[]{:T(128)} %constant.21.clone.1), window={size=1x1x128 pad=0_0x0_0x127_0}, to_apply=%region_0.1 | reduce-window | flops 8323072 | bytes 524292 | tf_op jit(solution)/shard_map/reduce-window
  26.1 8.2 %scatter_custom_fusion.4 = s32[6144]{0:T(1024)S(1)} fusion(s32[2048]{0:T(1024)S(1)} %broadcast_select_fusion.1, s32[2048]{0:T(1024)} %bitcast.222, s32[]{:T(128)} %constant.29.clone.1), kind=kCustom, calls=%fused_computation.78 | custom fusion | bytes 25088
  35.1 3.6 %all-to-all-start.3 = ((f32[8,4,2048]{2,0,1:T(8,128)}), f32[8,4,2048]{2,0,1:T(8,128)S(1)}, u32[]{:S(2)}, u32[]{:S(2)}) async-start(f32[8,4,2048]{2,0,1:T(8,128)} %bitcast.30), calls=%async_computation.3 | async-start | bytes 524288 | tf_op jit(solution)/shard_map/all_to_all | solution.py:19
  38.9 4.1 %all-to-all-done.3 = f32[8,4,2048]{2,0,1:T(8,128)S(1)} async-done(((f32[8,4,2048]{2,0,1:T(8,128)}), f32[8,4,2048]{2,0,1:T(8,128)S(1)}, u32[]{:S(2)}, u32[]{:S(2)}) %all-to-all-start.3) | async-done | bytes 262176 | tf_op jit(solution)/shard_map/all_to_all | solution.py:19
  43.0 4.1 %all-to-all-start.1 = ((f32[8,4,2048]{2,0,1:T(8,128)}), f32[8,4,2048]{2,0,1:T(8,128)}, u32[]{:S(2)}, u32[]{:S(2)}) async-start(f32[8,4,2048]{2,0,1:T(8,128)} %bitcast.2), calls=%async_computation.1 | async-start | bytes 524288 | tf_op jit(solution)/shard_map/all_to_all | solution.py:18
  47.2 10.6 %fusion.2 = f32[8,32,16,256]{3,1,2,0:T(8,128)} fusion(bf16[1,1,8,16,256,256]{5,4,3,2,1,0:T(8,128)(2,1)} %param.10, bf16[32,8,256,1]{2,1,0,3:T(8,128)(2,1)S(1)} %bitcast.214), kind=kOutput, calls=%fused_computation.10 | convolution fusion | flops 536870912 | bytes 21102592 | tf_op jit(solution)/shard_map/rkij,bri->brkj/dot_general | solution.py:51
  58.2 13.5 %scatter_fusion = f32[32,96,256]{2,0,1:T(8,128)S(1)} fusion(f32[32,96,256]{2,0,1:T(8,128)S(1)} %broadcast.223.clone, s32[128]{0:T(128)S(1)} %fusion.45, f32[128,32,256]{2,1,0:T(8,128)} %bitcast.195), kind=kCustom, calls=%fused_computation.2 | custom fusion | flops 1048576 | bytes 12583424 | tf_op jit(solution)/shard_map/scatter-add | solution.py:58
  80.1 3.8 %collective-permute-start.5 = (f32[32,4,2048]{2,1,0:T(4,128)}, f32[32,4,2048]{2,1,0:T(4,128)}, u32[]{:S(2)}, u32[]{:S(2)}) collective-permute-start(f32[32,4,2048]{2,1,0:T(4,128)} %get-tuple-element.19), channel_id=1, source_target_pairs={{7,0},{0,1},{1,2},{2,3},{3,4},{4,5},{5,6},{6,7},{15,8},{8,9},{9,10... | collective-permute-start | bytes 3145736 | tf_op jit(solution)/shard_map/ppermute | solution.py:10
  84.9 6.6 %all-to-all-start.2 = ((s32[1,32,192]{2,0,1:T(1,128)}), s32[1,32,192]{2,0,1:T(1,128)S(1)}, u32[]{:S(2)}, u32[]{:S(2)}) async-start(s32[1,32,192]{2,0,1:T(1,128)} %reshape.309), calls=%async_computation.2 | async-start | bytes 65536 | tf_op jit(solution)/shard_map/all_to_all | solution.py:102
  92.5 9.1 %all_gather.6 = bf16[32,8192]{1,0:T(8,128)(2,1)S(1)} all-gather(bf16[32,2048]{1,0:T(8,128)(2,1)S(1)} %fusion.38), channel_id=1, replica_groups=mesh['band'=4,'patch'=8] {'band'}, dimensions={1}, use_global_device_ids=true | all-gather | bytes 655360 | tf_op jit(solution)/shard_map/all_gather | solution.py:38
  108.2 5.3 %collective-permute-done = bf16[32,8192]{1,0:T(8,128)(2,1)S(1)} collective-permute-done((bf16[32,8192]{1,0:T(8,128)(2,1)S(1)}, bf16[32,8192]{1,0:T(8,128)(2,1)S(1)}, u32[]{:S(2)}, u32[]{:S(2)}) %collective-permute-start) | collective-permute-done | bytes 524320 | tf_op jit(solution)/shard_map/ppermute | solution.py:10
  113.5 5.5 %collective-permute-done.1 = bf16[32,8192]{1,0:T(8,128)(2,1)S(1)} collective-permute-done((bf16[32,8192]{1,0:T(8,128)(2,1)S(1)}, bf16[32,8192]{1,0:T(8,128)(2,1)S(1)}, u32[]{:S(2)}, u32[]{:S(2)}) %collective-permute-start.1) | collective-permute-done | bytes 524320 | tf_op jit(solution)/shard_map/ppermute | solution.py:10
  122.6 10.8 %fusion.10 = f32[8,4,8,256]{3,2,1,0:T(8,128)S(1)} fusion(bf16[32,8,16,256]{3,0,2,1:T(8,128)(2,1)S(1)} %bitcast.198, bf16[1,1,8,16,256,256]{5,4,3,2,1,0:T(8,128)(2,1)} %param.10), kind=kOutput, calls=%fused_computation.22 | convolution fusion | flops 536870912 | bytes 19136512 | tf_op jit(solution)/shard_map/rkij,brkj->bri/dot_general | solution.py:47
  137.0 10.6 %fusion = f32[8,32,16,256]{3,1,2,0:T(8,128)} fusion(bf16[1,1,8,16,256,256]{5,4,3,2,1,0:T(8,128)(2,1)} %param.10, bf16[32,8,256,1]{2,1,0,3:T(8,128)(2,1)S(1)} %bitcast.213), kind=kOutput, calls=%fused_computation.8 | convolution fusion | flops 536870912 | bytes 21102592 | tf_op jit(solution)/shard_map/rkij,bri->brkj/dot_general | solution.py:51
  147.9 13.5 %scatter_fusion.1 = f32[32,96,256]{2,0,1:T(8,128)S(1)} fusion(f32[32,96,256]{2,0,1:T(8,128)S(1)} %broadcast.223, s32[128]{0:T(128)S(1)} %fusion.45, f32[128,32,256]{2,1,0:T(8,128)} %bitcast.194), kind=kCustom, calls=%fused_computation.3 | custom fusion | flops 1048576 | bytes 12583424 | tf_op jit(solution)/shard_map/scatter-add | solution.py:58
  171.6 9.0 %all_gather.7 = bf16[32,8192]{1,0:T(8,128)(2,1)S(1)} all-gather(bf16[32,2048]{1,0:T(8,128)(2,1)S(1)} %fusion.33), channel_id=1, replica_groups=mesh['band'=4,'patch'=8] {'band'}, dimensions={1}, use_global_device_ids=true | all-gather | bytes 655360 | tf_op jit(solution)/shard_map/all_gather | solution.py:38
  189.7 7.9 %collective-permute-done.2 = bf16[32,8192]{1,0:T(8,128)(2,1)S(1)} collective-permute-done((bf16[32,8192]{1,0:T(8,128)(2,1)S(1)}, bf16[32,8192]{1,0:T(8,128)(2,1)S(1)}, u32[]{:S(2)}, u32[]{:S(2)}) %collective-permute-start.2) | collective-permute-done | bytes 524320 | tf_op jit(solution)/shard_map/ppermute | solution.py:10
  203.9 11.0 %fusion.4 = f32[8,32,256,1]{2,1,3,0:T(8,128)S(1)} fusion(bf16[32,8,16,256]{3,0,2,1:T(8,128)(2,1)S(1)} %bitcast.197, bf16[1,1,8,16,256,256]{5,4,3,2,1,0:T(8,128)(2,1)} %param.10), kind=kOutput, calls=%fused_computation.12 | convolution fusion | flops 536870912 | bytes 19136512 | tf_op jit(solution)/shard_map/rkij,brkj->bri/dot_general | solution.py:47
  214.9 5.2 %reduce-scatter.9.cloned.1.call-done = f32[32,1,2048]{2,0,1:T(8,128)} async-done(((f32[32,4,2048]{2,0,1:T(8,128)}), f32[32,1,2048]{2,0,1:T(8,128)}) %reduce-scatter.9.cloned.1.call-update) | async-done | bytes 262160
  222.7 6.7 %scatter_custom_fusion.5 = f32[32,6144]{0,1:T(8,128)S(1)} fusion(s32[2048]{0:T(1024)S(1)} %broadcast_select_fusion, f32[2048,32]{1,0:T(8,128)} %copy.112, f32[]{:T(128)} %constant.25.clone.1), kind=kCustom, calls=%fused_computation.20 | custom fusion | bytes 786944
  231.6 5.1 %all-to-all-start.4 = ((f32[32,32,192]{2,0,1:T(8,128)}), f32[32,32,192]{2,0,1:T(8,128)S(1)}, u32[]{:S(2)}, u32[]{:S(2)}) async-start(f32[32,32,192]{2,0,1:T(8,128)} %copy.113), calls=%async_computation.4 | async-start | bytes 2097152 | tf_op jit(solution)/shard_map/all_to_all | solution.py:101
  236.9 42.6 %scatter_custom_fusion.3 = f32[1025]{0:T(1024)S(1)} fusion(s32[6144]{0:T(1024)S(1)} %reshape.348, f32[6144]{0:T(1024)S(1)} %broadcast.242, f32[]{:T(128)} %constant.25.clone.1), kind=kCustom, calls=%fused_computation.87 | custom fusion | flops 6144 | bytes 4104 | tf_op jit(solution)/shard_map/scatter-add | solution.py:109
  286.5 41.4 %scatter_custom_fusion.2 = f32[1025,32]{1,0:T(8,128)} fusion(s32[6144]{0:T(1024)S(1)} %reshape.348, f32[6144,32]{1,0:T(8,128)S(1)} %copy.115, f32[]{:T(128)} %constant.25.clone.1), kind=kCustom, calls=%fused_computation.37 | custom fusion | flops 196608 | bytes 131204 | tf_op jit(solution)/shard_map/scatter-add | solution.py:106
  (106 shorter events, 70.9 us)
Async XLA Ops:
  7.2 18.8 %copy-start.7 = (s32[3]{0:T(128)S(1)}, s32[3]{0:T(128)}, u32[]{:S(2)}) copy-start(s32[3]{0:T(128)} %constant.59) | copy-start | bytes 40
  7.2 18.9 %copy-start.8 = (s32[3]{0:T(128)S(1)}, s32[3]{0:T(128)}, u32[]{:S(2)}) copy-start(s32[3]{0:T(128)} %constant.62) | copy-start | bytes 40
  7.2 27.9 %all-to-all-start = ((f32[8,4,2048]{2,0,1:T(8,128)}), f32[8,4,2048]{2,0,1:T(8,128)S(1)}, u32[]{:S(2)}, u32[]{:S(2)}) async-start(f32[8,4,2048]{2,0,1:T(8,128)} %bitcast.215), calls=%async_computation | async-start | bytes 524288 | tf_op jit(solution)/shard_map/all_to_all | solution.py:17
  35.1 7.9 %all-to-all-start.3 = ((f32[8,4,2048]{2,0,1:T(8,128)}), f32[8,4,2048]{2,0,1:T(8,128)S(1)}, u32[]{:S(2)}, u32[]{:S(2)}) async-start(f32[8,4,2048]{2,0,1:T(8,128)} %bitcast.30), calls=%async_computation.3 | async-start | bytes 524288 | tf_op jit(solution)/shard_map/all_to_all | solution.py:19
  38.9 18.9 %copy-start.5 = (f32[4,8,8,256]{3,2,1,0:T(8,128)}, f32[4,8,8,256]{3,2,1,0:T(8,128)S(1)}, u32[]{:S(2)}) copy-start(f32[4,8,8,256]{3,2,1,0:T(8,128)S(1)} %copy.135) | copy-start | bytes 786436
  43.0 14.8 %copy-start.3 = (f32[8,4,2048]{2,0,1:T(8,128)}, f32[8,4,2048]{2,0,1:T(8,128)S(1)}, u32[]{:S(2)}) copy-start(f32[8,4,2048]{2,0,1:T(8,128)S(1)} %all-to-all-done.3) | copy-start | bytes 786436
  43.0 41.9 %all-to-all-start.1 = ((f32[8,4,2048]{2,0,1:T(8,128)}), f32[8,4,2048]{2,0,1:T(8,128)}, u32[]{:S(2)}, u32[]{:S(2)}) async-start(f32[8,4,2048]{2,0,1:T(8,128)} %bitcast.2), calls=%async_computation.1 | async-start | bytes 524288 | tf_op jit(solution)/shard_map/all_to_all | solution.py:18
  80.1 24.3 %collective-permute-start.5 = (f32[32,4,2048]{2,1,0:T(4,128)}, f32[32,4,2048]{2,1,0:T(4,128)}, u32[]{:S(2)}, u32[]{:S(2)}) collective-permute-start(f32[32,4,2048]{2,1,0:T(4,128)} %get-tuple-element.19), channel_id=1, source_target_pairs={{7,0},{0,1},{1,2},{2,3},{3,4},{4,5},{5,6},{6,7},{15,8},{8,9},{9,10... | collective-permute-start | bytes 3145736 | tf_op jit(solution)/shard_map/ppermute | solution.py:10
  84.9 19.5 %collective-permute-start.4 = (bf16[32,4,2048]{2,1,0:T(4,128)(2,1)}, bf16[32,4,2048]{2,1,0:T(4,128)(2,1)S(1)}, u32[]{:S(2)}, u32[]{:S(2)}) collective-permute-start(bf16[32,4,2048]{2,1,0:T(4,128)(2,1)} %fusion.17), channel_id=1, source_target_pairs={{1,0},{2,1},{3,2},{4,3},{5,4},{6,5},{7,6},{0,7},{9,8},{10,9},{11,1... | collective-permute-start | bytes 1572872 | tf_op jit(solution)/shard_map/ppermute | solution.py:10
  84.9 146.7 %all-to-all-start.2 = ((s32[1,32,192]{2,0,1:T(1,128)}), s32[1,32,192]{2,0,1:T(1,128)S(1)}, u32[]{:S(2)}, u32[]{:S(2)}) async-start(s32[1,32,192]{2,0,1:T(1,128)} %reshape.309), calls=%async_computation.2 | async-start | bytes 65536 | tf_op jit(solution)/shard_map/all_to_all | solution.py:102
  91.5 44.4 %reduce-scatter.7.cloned.1.call-start = ((), (), s32[]{:S(2)}) async-start(), calls=%async_computation.7 | async-start | bytes 1310720
  101.6 11.9 %collective-permute-start = (bf16[32,8192]{1,0:T(8,128)(2,1)S(1)}, bf16[32,8192]{1,0:T(8,128)(2,1)S(1)}, u32[]{:S(2)}, u32[]{:S(2)}) collective-permute-start(bf16[32,8192]{1,0:T(8,128)(2,1)S(1)} %all_gather.6), channel_id=1, source_target_pairs={{7,0},{0,1},{1,2},{2,3},{3,4},{4,5},{5,6},{6,7},{15,8},{8,9},{9,10... | collective-permute-start | bytes 1572872 | tf_op jit(solution)/shard_map/ppermute | solution.py:10
  104.4 14.6 %collective-permute-start.1 = (bf16[32,8192]{1,0:T(8,128)(2,1)S(1)}, bf16[32,8192]{1,0:T(8,128)(2,1)S(1)}, u32[]{:S(2)}, u32[]{:S(2)}) collective-permute-start(bf16[32,8192]{1,0:T(8,128)(2,1)S(1)} %all_gather.6), channel_id=1, source_target_pairs={{1,0},{2,1},{3,2},{4,3},{5,4},{6,5},{7,6},{0,7},{9,8},{10,9},{11,1... | collective-permute-start | bytes 1572872 | tf_op jit(solution)/shard_map/ppermute | solution.py:10
  108.0 112.1 %reduce-scatter.9.cloned.1.call-start = ((), (), s32[]{:S(2)}) async-start(), calls=%async_computation.8 | async-start | bytes 1310720
  122.6 14.4 %copy-start.6 = (f32[4,8,8,256]{3,2,1,0:T(8,128)S(1)}, f32[4,8,8,256]{3,2,1,0:T(8,128)}, u32[]{:S(2)}) copy-start(f32[4,8,8,256]{3,2,1,0:T(8,128)} %copy-done.5) | copy-start | bytes 786436
  168.3 2.3 copy-start.1
  168.5 19.2 %collective-permute-start.7 = (f32[32,4,2048]{2,1,0:T(4,128)S(1)}, f32[32,4,2048]{2,1,0:T(4,128)S(1)}, u32[]{:S(2)}, u32[]{:S(2)}) collective-permute-start(f32[32,4,2048]{2,1,0:T(4,128)S(1)} %get-tuple-element.17), channel_id=1, source_target_pairs={{7,0},{0,1},{1,2},{2,3},{3,4},{4,5},{5,6},{6,7},{15,8},{8,9},{9,10... | collective-permute-start | bytes 3145736 | tf_op jit(solution)/shard_map/ppermute | solution.py:10
  170.5 16.5 %collective-permute-start.6 = (bf16[32,4,2048]{2,1,0:T(4,128)(2,1)S(1)}, bf16[32,4,2048]{2,1,0:T(4,128)(2,1)S(1)}, u32[]{:S(2)}, u32[]{:S(2)}) collective-permute-start(bf16[32,4,2048]{2,1,0:T(4,128)(2,1)S(1)} %fusion.18), channel_id=1, source_target_pairs={{1,0},{2,1},{3,2},{4,3},{5,4},{6,5},{7,6},{0,7},{9,8},{10,9},{11,1... | collective-permute-start | bytes 1572872 | tf_op jit(solution)/shard_map/ppermute | solution.py:10
  180.7 16.9 %collective-permute-start.2 = (bf16[32,8192]{1,0:T(8,128)(2,1)S(1)}, bf16[32,8192]{1,0:T(8,128)(2,1)S(1)}, u32[]{:S(2)}, u32[]{:S(2)}) collective-permute-start(bf16[32,8192]{1,0:T(8,128)(2,1)S(1)} %all_gather.7), channel_id=1, source_target_pairs={{7,0},{0,1},{1,2},{2,3},{3,4},{4,5},{5,6},{6,7},{15,8},{8,9},{9,10... | collective-permute-start | bytes 1572872 | tf_op jit(solution)/shard_map/ppermute | solution.py:10
  183.3 16.9 %collective-permute-start.3 = (bf16[32,8192]{1,0:T(8,128)(2,1)S(1)}, bf16[32,8192]{1,0:T(8,128)(2,1)S(1)}, u32[]{:S(2)}, u32[]{:S(2)}) collective-permute-start(bf16[32,8192]{1,0:T(8,128)(2,1)S(1)} %all_gather.7), channel_id=1, source_target_pairs={{1,0},{2,1},{3,2},{4,3},{5,4},{6,5},{7,6},{0,7},{9,8},{10,9},{11,1... | collective-permute-start | bytes 1572872 | tf_op jit(solution)/shard_map/ppermute | solution.py:10
  203.9 16.2 %copy-start.2 = (f32[8,4,8,256]{3,2,0,1:T(8,128)S(1)}, f32[8,4,8,256]{3,2,0,1:T(8,128)}, u32[]{:S(2)}) copy-start(f32[8,4,8,256]{3,2,0,1:T(8,128)} %copy.133) | copy-start | bytes 786436
  203.9 16.2 %copy-start.4 = (f32[8,4,2048]{2,0,1:T(8,128)S(1)}, f32[8,4,2048]{2,0,1:T(8,128)}, u32[]{:S(2)}) copy-start(f32[8,4,2048]{2,0,1:T(8,128)} %copy-done.3) | copy-start | bytes 786436
  214.9 6.4 %copy-start = (f32[8,32,256,1]{2,1,3,0:T(8,128)}, f32[8,32,256,1]{2,1,3,0:T(8,128)S(1)}, u32[]{:S(2)}) copy-start(f32[8,32,256,1]{2,1,3,0:T(8,128)S(1)} %fusion.4) | copy-start | bytes 786436
  231.6 51.1 %all-to-all-start.4 = ((f32[32,32,192]{2,0,1:T(8,128)}), f32[32,32,192]{2,0,1:T(8,128)S(1)}, u32[]{:S(2)}, u32[]{:S(2)}) async-start(f32[32,32,192]{2,0,1:T(8,128)} %copy.113), calls=%async_computation.4 | async-start | bytes 2097152 | tf_op jit(solution)/shard_map/all_to_all | solution.py:101
Sparse Core Ops, SparseCore 0:
  108.1 27.7 reduce-scatter.6
  189.9 30.2 reduce-scatter.8
where the time goes:
time: 339 us; the launch traced here: 337 us
  other arithmetic  133 us (39%)
  local copies, waits for them, and re-layouts  56.2 us (17%)
  matrix products  43 us (13%)
  starting transfers between devices  36.7 us (11%)
  waiting for transfers between devices  35.1 us (10%)
  blocking collectives  18.1 us (5%)
  between operations  14.5 us (4%)
    scatter-add x1, other arithmetic, body(): jax.ops.segment_sum(jnp.ones((device_count * capacity,), jnp.float32), fl...  42.6 us
    scatter-add x1, other arithmetic, body(): jax.ops.segment_sum(flat_values.T, flat_labels, surface_count + 1)  41.4 us
    scatter-add x2, other arithmetic, adjoint(): empty.at[:, flat_offsets]  26.9 us
    ppermute x8, waiting for transfers between devices, passed_along(): return lax.ppermute(block, axis, route)  24 us
    dot_general x2, matrix products, forward(): jnp.einsum('rkij,brkj->bri', matrix, picked, preferred_element_type=jnp.f...  21.8 us
    dot_general x2, matrix products, adjoint(): jnp.einsum('rkij,bri->brkj', matrix, vector.reshape(band_count, rb_count,...  21.2 us
    all_gather x2, blocking collectives, window(): gathered = lax.all_gather(vector, 'band', axis=1, tiled=True)  18.1 us
    unnamed x25, local copies, waits for them, and re-layouts  18 us
  transfers between devices with their start and end apart: 15, of which 9 were waited for; matrix products, arithmetic and copies ran while one was open for 55% of the time, Pallas kernels for 0%

commit v1 on v0

--- a/solution.py
+++ b/solution.py
@@ -35,7 +35,16 @@
     reflect = 1.0 - emissive
 
     def window(vector):
-        gathered = lax.all_gather(vector, "band", axis=1, tiled=True)
+        array = vector
+        ways, here, turn = (lax.axis_size("band"), lax.axis_index("band"), array.shape[1])
+        lengths = [n * ways if d == 1 else n for d, n in enumerate(array.shape)]
+        full = lax.dynamic_update_slice_in_dim(
+            jnp.zeros(lengths, array.dtype), array, here * turn, axis=1
+        )
+        for far in range(1, ways):
+            array = lax.ppermute(array, "band", [(d, (d + 1) % ways) for d in range(ways)])
+            full = lax.dynamic_update_slice_in_dim(full, array, (here - far) % ways * turn, axis=1)
+        gathered = full
         lower_rows = passed_along(gathered, "patch", 1)
         upper_rows = passed_along(gathered, "patch", -1)
         joined = jnp.concatenate([lower_rows, gathered, upper_rows], axis=1)

time: 339 us -> 353 us (1.041)
  waiting for transfers between devices: 35.1 us -> 57.2 us
  blocking collectives: 18.1 us -> 0 us
  starting transfers between devices: 36.7 us -> 43.3 us
  local copies, waits for them, and re-layouts: 56.2 us -> 60.4 us
    all_gather x2 -> x0, blocking collectives: 18.1 us -> none  [window(): gathered = lax.all_gather(vector, 'band', axis=1, tiled=True)]
    ppermute x0 -> x6, waiting for transfers between devices: none -> 13.2 us  [window(): lax.ppermute(array, 'band', [(d, (d + 1) % ways) for d in range(ways)])]
    ppermute x0 -> x6, starting transfers between devices: none -> 5.37 us  [window(): lax.ppermute(array, 'band', [(d, (d + 1) % ways) for d in range(ways)])]
    dynamic_update_slice x0 -> x6, local copies, waits for them, and re-layouts: none -> 5.09 us  [window(): lax.dynamic_update_slice_in_dim(full, array, (here - far) % ways * turn,...]
    ppermute x8, waiting for transfers between devices: 24 us -> 28.7 us  [passed_along(): return lax.ppermute(block, axis, route)]
    all_to_all x1, waiting for transfers between devices: 0.01 us -> 3.67 us  [body(): lax.all_to_all(blackbody, 'band', split_axis=1, concat_axis=0, tiled=True)]
    unnamed x4, waiting for transfers between devices: 6.97 us -> 10.6 us
    unnamed x25 -> x41, local copies, waits for them, and re-layouts: 18 us -> 18.3 us
  transfers between devices with their start and end apart: 15 -> 21, of which waited for: 9 -> 14; matrix products, arithmetic and copies ran while one was open for 55% -> 54% of each run, Pallas kernels for 0% -> 0%
where the time goes in v1:
time: 353 us; the launch traced here: 351 us
  other arithmetic  132 us (37%)
  local copies, waits for them, and re-layouts  60.4 us (17%)
  waiting for transfers between devices  57.2 us (16%)
  starting transfers between devices  43.3 us (12%)
  matrix products  43.2 us (12%)
  between operations  14.6 us (4%)
    scatter-add x1, other arithmetic, body(): jax.ops.segment_sum(jnp.ones((device_count * capacity,), jnp.float32), fl...  42.6 us
    scatter-add x1, other arithmetic, body(): jax.ops.segment_sum(flat_values.T, flat_labels, surface_count + 1)  41.4 us
    ppermute x8, waiting for transfers between devices, passed_along(): return lax.ppermute(block, axis, route)  28.7 us
    scatter-add x2, other arithmetic, adjoint(): empty.at[:, flat_offsets]  27 us
    dot_general x2, matrix products, forward(): jnp.einsum('rkij,brkj->bri', matrix, picked, preferred_element_type=jnp.f...  22 us
    dot_general x2, matrix products, adjoint(): jnp.einsum('rkij,bri->brkj', matrix, vector.reshape(band_count, rb_count,...  21.2 us
    unnamed x41, local copies, waits for them, and re-layouts  18.3 us
    ppermute x6, waiting for transfers between devices, window(): lax.ppermute(array, 'band', [(d, (d + 1) % ways) for d in range(ways)])  13.2 us
  transfers between devices with their start and end apart: 21, of which 14 were waited for; matrix products, arithmetic and copies ran while one was open for 54% of the time, Pallas kernels for 0%

profile of v1, /device:TPU:1, one launch (start us, length us, event | category | flops | bytes accessed | tf_op | source)
XLA Modules:
  0.0 350.9 jit_solution(926004179304569636)
XLA Ops:
  7.2 4.4 %all-to-all-start = ((f32[8,4,2048]{2,0,1:T(8,128)}), f32[8,4,2048]{2,0,1:T(8,128)S(1)}, u32[]{:S(2)}, u32[]{:S(2)}) async-start(f32[8,4,2048]{2,0,1:T(8,128)} %bitcast.219), calls=%async_computation | async-start | bytes 524288 | tf_op jit(solution)/shard_map/all_to_all | solution.py:17
  13.2 9.1 %reduce-window.6 = s32[32,16,128]{2,1,0:T(8,128)S(1)} reduce-window(s32[32,16,128]{2,1,0:T(8,128)S(1)} %fusion.35, s32[]{:T(128)} %constant.81.clone.1), window={size=1x1x128 pad=0_0x0_0x127_0}, to_apply=%region_0.1 | reduce-window | flops 8323072 | bytes 524292 | tf_op jit(solution)/shard_map/reduce-window
  24.2 8.2 %scatter_custom_fusion.4 = s32[6144]{0:T(1024)S(1)} fusion(s32[2048]{0:T(1024)S(1)} %broadcast_select_fusion.1, s32[2048]{0:T(1024)} %bitcast.226, s32[]{:T(128)} %constant.96.clone.1), kind=kCustom, calls=%fused_computation.78 | custom fusion | bytes 25088
  33.3 3.6 %all-to-all-start.1 = ((f32[8,4,2048]{2,0,1:T(8,128)}), f32[8,4,2048]{2,0,1:T(8,128)S(1)}, u32[]{:S(2)}, u32[]{:S(2)}) async-start(f32[8,4,2048]{2,0,1:T(8,128)} %bitcast.2), calls=%async_computation.1 | async-start | bytes 524288 | tf_op jit(solution)/shard_map/all_to_all | solution.py:18
  37.5 3.7 %all-to-all-done.1 = f32[8,4,2048]{2,0,1:T(8,128)S(1)} async-done(((f32[8,4,2048]{2,0,1:T(8,128)}), f32[8,4,2048]{2,0,1:T(8,128)S(1)}, u32[]{:S(2)}, u32[]{:S(2)}) %all-to-all-start.1) | async-done | bytes 262176 | tf_op jit(solution)/shard_map/all_to_all | solution.py:18
  48.8 9.4 %all-to-all-start.2 = ((s32[1,32,192]{2,0,1:T(1,128)}), s32[1,32,192]{2,0,1:T(1,128)}, u32[]{:S(2)}, u32[]{:S(2)}) async-start(s32[1,32,192]{2,0,1:T(1,128)} %reshape.309), calls=%async_computation.2 | async-start | bytes 65536 | tf_op jit(solution)/shard_map/all_to_all | solution.py:111
  58.3 10.6 %fusion.2 = f32[8,32,16,256]{3,1,2,0:T(8,128)} fusion(bf16[1,1,8,16,256,256]{5,4,3,2,1,0:T(8,128)(2,1)} %param.10, bf16[32,8,256,1]{2,1,0,3:T(8,128)(2,1)S(1)} %bitcast.218), kind=kOutput, calls=%fused_computation.10 | convolution fusion | flops 536870912 | bytes 21102592 | tf_op jit(solution)/shard_map/rkij,bri->brkj/dot_general | solution.py:60
  69.3 13.6 %scatter_fusion = f32[32,96,256]{2,0,1:T(8,128)S(1)} fusion(f32[32,96,256]{2,0,1:T(8,128)S(1)} %broadcast.230.clone, s32[128]{0:T(128)} %fusion.45, f32[128,32,256]{2,1,0:T(8,128)} %bitcast.199), kind=kCustom, calls=%fused_computation.2 | custom fusion | flops 1048576 | bytes 12583424 | tf_op jit(solution)/shard_map/scatter-add | solution.py:67
  98.0 4.0 %collective-permute-done.2 = bf16[32,2048]{1,0:T(8,128)(2,1)S(1)} collective-permute-done((bf16[32,2048]{1,0:T(8,128)(2,1)S(1)}, bf16[32,2048]{1,0:T(8,128)(2,1)S(1)}, u32[]{:S(2)}, u32[]{:S(2)}) %collective-permute-start.2) | collective-permute-done | bytes 131104 | tf_op jit(solution)/shard_map/ppermute | solution.py:45
  102.7 3.7 %collective-permute-start.3 = (bf16[32,8192]{1,0:T(8,128)(2,1)}, bf16[32,8192]{1,0:T(8,128)(2,1)S(1)}, u32[]{:S(2)}, u32[]{:S(2)}) collective-permute-start(bf16[32,8192]{1,0:T(8,128)(2,1)} %constant_dynamic-update-slice_fusion.4), channel_id=1, source_target_pairs={{7,0},{0,1},{1,2},{2,3},{3,4},{4,5},{5,6},{6,7},{15,8},{8,9},{9,10... | collective-permute-start | bytes 1572872 | tf_op jit(solution)/shard_map/ppermute | solution.py:10
  111.3 6.9 %collective-permute-done.3 = bf16[32,8192]{1,0:T(8,128)(2,1)S(1)} collective-permute-done((bf16[32,8192]{1,0:T(8,128)(2,1)}, bf16[32,8192]{1,0:T(8,128)(2,1)S(1)}, u32[]{:S(2)}, u32[]{:S(2)}) %collective-permute-start.3) | collective-permute-done | bytes 524320 | tf_op jit(solution)/shard_map/ppermute | solution.py:10
  118.2 4.5 %collective-permute-done.4 = bf16[32,8192]{1,0:T(8,128)(2,1)S(1)} collective-permute-done((bf16[32,8192]{1,0:T(8,128)(2,1)}, bf16[32,8192]{1,0:T(8,128)(2,1)S(1)}, u32[]{:S(2)}, u32[]{:S(2)}) %collective-permute-start.4) | collective-permute-done | bytes 524320 | tf_op jit(solution)/shard_map/ppermute | solution.py:10
  127.4 10.9 %fusion.10 = f32[8,4,8,256]{3,2,1,0:T(8,128)S(1)} fusion(bf16[32,8,16,256]{3,0,2,1:T(8,128)(2,1)S(1)} %bitcast.202, bf16[1,1,8,16,256,256]{5,4,3,2,1,0:T(8,128)(2,1)} %param.10), kind=kOutput, calls=%fused_computation.22 | convolution fusion | flops 536870912 | bytes 19136512 | tf_op jit(solution)/shard_map/rkij,brkj->bri/dot_general | solution.py:56
  140.5 4.9 %collective-permute-done.5 = bf16[32,2048]{1,0:T(8,128)(2,1)S(1)} collective-permute-done((bf16[32,2048]{1,0:T(8,128)(2,1)S(1)}, bf16[32,2048]{1,0:T(8,128)(2,1)S(1)}, u32[]{:S(2)}, u32[]{:S(2)}) %collective-permute-start.5) | collective-permute-done | bytes 131104 | tf_op jit(solution)/shard_map/ppermute | solution.py:45
  146.5 10.6 %fusion = f32[8,32,16,256]{3,1,2,0:T(8,128)} fusion(bf16[1,1,8,16,256,256]{5,4,3,2,1,0:T(8,128)(2,1)} %param.10, bf16[32,8,256,1]{2,1,0,3:T(8,128)(2,1)S(1)} %bitcast.217), kind=kOutput, calls=%fused_computation.8 | convolution fusion | flops 536870912 | bytes 21102592 | tf_op jit(solution)/shard_map/rkij,bri->brkj/dot_general | solution.py:60
  157.7 13.5 %scatter_fusion.1 = f32[32,96,256]{2,0,1:T(8,128)S(1)} fusion(f32[32,96,256]{2,0,1:T(8,128)S(1)} %broadcast.230, s32[128]{0:T(128)S(1)} %copy-done.12, f32[128,32,256]{2,1,0:T(8,128)} %bitcast.198), kind=kCustom, calls=%fused_computation.3 | custom fusion | flops 1048576 | bytes 12583424 | tf_op jit(solution)/shard_map/scatter-add | solution.py:67
  193.6 4.3 %collective-permute-done.13 = f32[32,4,2048]{2,1,0:T(4,128)S(1)} collective-permute-done((f32[32,4,2048]{2,1,0:T(4,128)S(1)}, f32[32,4,2048]{2,1,0:T(4,128)S(1)}, u32[]{:S(2)}, u32[]{:S(2)}) %collective-permute-start.13) | collective-permute-done | bytes 1048608 | tf_op jit(solution)/shard_map/ppermute | solution.py:10
  200.0 8.2 %collective-permute-done.8 = bf16[32,8192]{1,0:T(8,128)(2,1)S(1)} collective-permute-done((bf16[32,8192]{1,0:T(8,128)(2,1)}, bf16[32,8192]{1,0:T(8,128)(2,1)S(1)}, u32[]{:S(2)}, u32[]{:S(2)}) %collective-permute-start.8) | collective-permute-done | bytes 524320 | tf_op jit(solution)/shard_map/ppermute | solution.py:10
  212.8 11.1 %fusion.4 = f32[8,32,256,1]{2,1,3,0:T(8,128)S(1)} fusion(bf16[32,8,16,256]{3,0,2,1:T(8,128)(2,1)S(1)} %bitcast.201, bf16[1,1,8,16,256,256]{5,4,3,2,1,0:T(8,128)(2,1)} %param.10), kind=kOutput, calls=%fused_computation.12 | convolution fusion | flops 536870912 | bytes 19136512 | tf_op jit(solution)/shard_map/rkij,brkj->bri/dot_general | solution.py:56
  224.0 10.5 %reduce-scatter.9.cloned.1.call-done = f32[32,1,2048]{2,0,1:T(8,128)} async-done(((f32[32,4,2048]{2,0,1:T(8,128)}), f32[32,1,2048]{2,0,1:T(8,128)}) %reduce-scatter.9.cloned.1.call-update) | async-done | bytes 262160
  237.0 6.7 %scatter_custom_fusion.5 = f32[32,6144]{0,1:T(8,128)S(1)} fusion(s32[2048]{0:T(1024)} %broadcast_select_fusion, f32[2048,32]{1,0:T(8,128)} %copy.90, f32[]{:T(128)} %constant.95.clone.1), kind=kCustom, calls=%fused_computation.20 | custom fusion | bytes 786944
  245.9 5.0 %all-to-all-start.4 = ((f32[32,32,192]{2,0,1:T(8,128)}), f32[32,32,192]{2,0,1:T(8,128)S(1)}, u32[]{:S(2)}, u32[]{:S(2)}) async-start(f32[32,32,192]{2,0,1:T(8,128)} %copy.91), calls=%async_computation.4 | async-start | bytes 2097152 | tf_op jit(solution)/shard_map/all_to_all | solution.py:110
  251.8 42.6 %scatter_custom_fusion.3 = f32[1025]{0:T(1024)S(1)} fusion(s32[6144]{0:T(1024)S(1)} %reshape.348, f32[6144]{0:T(1024)S(1)} %broadcast.249, f32[]{:T(128)} %constant.95.clone.1), kind=kCustom, calls=%fused_computation.87 | custom fusion | flops 6144 | bytes 4104 | tf_op jit(solution)/shard_map/scatter-add | solution.py:118
  300.6 41.4 %scatter_custom_fusion.2 = f32[1025,32]{1,0:T(8,128)} fusion(s32[6144]{0:T(1024)S(1)} %reshape.348, f32[6144,32]{1,0:T(8,128)S(1)} %copy.93, f32[]{:T(128)} %constant.95.clone.1), kind=kCustom, calls=%fused_computation.37 | custom fusion | flops 196608 | bytes 131204 | tf_op jit(solution)/shard_map/scatter-add | solution.py:115
  (140 shorter events, 84.9 us)
Async XLA Ops:
  7.2 26.0 %copy-start.14 = (s32[2]{0:T(128)S(1)}, s32[2]{0:T(128)}, u32[]{:S(2)}) copy-start(s32[2]{0:T(128)} %constant.111) | copy-start | bytes 28
  7.2 26.1 %all-to-all-start = ((f32[8,4,2048]{2,0,1:T(8,128)}), f32[8,4,2048]{2,0,1:T(8,128)S(1)}, u32[]{:S(2)}, u32[]{:S(2)}) async-start(f32[8,4,2048]{2,0,1:T(8,128)} %bitcast.219), calls=%async_computation | async-start | bytes 524288 | tf_op jit(solution)/shard_map/all_to_all | solution.py:17
  33.3 7.9 %all-to-all-start.1 = ((f32[8,4,2048]{2,0,1:T(8,128)}), f32[8,4,2048]{2,0,1:T(8,128)S(1)}, u32[]{:S(2)}, u32[]{:S(2)}) async-start(f32[8,4,2048]{2,0,1:T(8,128)} %bitcast.2), calls=%async_computation.1 | async-start | bytes 524288 | tf_op jit(solution)/shard_map/all_to_all | solution.py:18
  41.2 27.8 %copy-start = (f32[8,4,2048]{2,0,1:T(8,128)}, f32[8,4,2048]{2,0,1:T(8,128)S(1)}, u32[]{:S(2)}) copy-start(f32[8,4,2048]{2,0,1:T(8,128)S(1)} %all-to-all-done.1) | copy-start | bytes 786436
  41.2 7.6 %all-to-all-start.3 = ((f32[8,4,2048]{2,0,1:T(8,128)}), f32[8,4,2048]{2,0,1:T(8,128)S(1)}, u32[]{:S(2)}, u32[]{:S(2)}) async-start(f32[8,4,2048]{2,0,1:T(8,128)} %bitcast.30), calls=%async_computation.3 | async-start | bytes 524288 | tf_op jit(solution)/shard_map/all_to_all | solution.py:19
  46.2 45.8 %collective-permute-start = (bf16[32,2048]{1,0:T(8,128)(2,1)}, bf16[32,2048]{1,0:T(8,128)(2,1)S(1)}, u32[]{:S(2)}, u32[]{:S(2)}) collective-permute-start(bf16[32,2048]{1,0:T(8,128)(2,1)} %get-tuple-element.17), channel_id=1, source_target_pairs={{0,8},{8,16},{16,24},{24,0},{1,9},{9,17},{17,25},{25,1},{2,10},{10... | collective-permute-start | bytes 393224 | tf_op jit(solution)/shard_map/ppermute | solution.py:45
  48.8 197.1 %all-to-all-start.2 = ((s32[1,32,192]{2,0,1:T(1,128)}), s32[1,32,192]{2,0,1:T(1,128)}, u32[]{:S(2)}, u32[]{:S(2)}) async-start(s32[1,32,192]{2,0,1:T(1,128)} %reshape.309), calls=%async_computation.2 | async-start | bytes 65536 | tf_op jit(solution)/shard_map/all_to_all | solution.py:111
  58.1 87.2 %reduce-scatter.7.cloned.1.call-start = ((), (), s32[]{:S(2)}) async-start(), calls=%async_computation.7 | async-start | bytes 1310720
  90.0 19.0 %collective-permute-start.11 = (f32[32,4,2048]{2,1,0:T(4,128)S(1)}, f32[32,4,2048]{2,1,0:T(4,128)S(1)}, u32[]{:S(2)}, u32[]{:S(2)}) collective-permute-start(f32[32,4,2048]{2,1,0:T(4,128)S(1)} %get-tuple-element.21), channel_id=1, source_target_pairs={{7,0},{0,1},{1,2},{2,3},{3,4},{4,5},{5,6},{6,7},{15,8},{8,9},{9,10... | collective-permute-start | bytes 3145736 | tf_op jit(solution)/shard_map/ppermute | solution.py:10
  91.9 16.5 %collective-permute-start.10 = (bf16[32,4,2048]{2,1,0:T(4,128)(2,1)S(1)}, bf16[32,4,2048]{2,1,0:T(4,128)(2,1)S(1)}, u32[]{:S(2)}, u32[]{:S(2)}) collective-permute-start(bf16[32,4,2048]{2,1,0:T(4,128)(2,1)S(1)} %fusion.17), channel_id=1, source_target_pairs={{1,0},{2,1},{3,2},{4,3},{5,4},{6,5},{7,6},{0,7},{9,8},{10,9},{11,1... | collective-permute-start | bytes 1572872 | tf_op jit(solution)/shard_map/ppermute | solution.py:10
  91.9 5.1 %collective-permute-start.1 = (bf16[32,2048]{1,0:T(8,128)(2,1)S(1)}, bf16[32,2048]{1,0:T(8,128)(2,1)S(1)}, u32[]{:S(2)}, u32[]{:S(2)}) collective-permute-start(bf16[32,2048]{1,0:T(8,128)(2,1)S(1)} %collective-permute-done), channel_id=1, source_target_pairs={{0,8},{8,16},{16,24},{24,0},{1,9},{9,17},{17,25},{25,1},{2,10},{10... | collective-permute-start | bytes 393224 | tf_op jit(solution)/shard_map/ppermute | solution.py:45
  97.0 5.0 %collective-permute-start.2 = (bf16[32,2048]{1,0:T(8,128)(2,1)S(1)}, bf16[32,2048]{1,0:T(8,128)(2,1)S(1)}, u32[]{:S(2)}, u32[]{:S(2)}) collective-permute-start(bf16[32,2048]{1,0:T(8,128)(2,1)S(1)} %collective-permute-done.1), channel_id=1, source_target_pairs={{0,8},{8,16},{16,24},{24,0},{1,9},{9,17},{17,25},{25,1},{2,10},{10... | collective-permute-start | bytes 393224 | tf_op jit(solution)/shard_map/ppermute | solution.py:45
  102.7 15.5 %collective-permute-start.3 = (bf16[32,8192]{1,0:T(8,128)(2,1)}, bf16[32,8192]{1,0:T(8,128)(2,1)S(1)}, u32[]{:S(2)}, u32[]{:S(2)}) collective-permute-start(bf16[32,8192]{1,0:T(8,128)(2,1)} %constant_dynamic-update-slice_fusion.4), channel_id=1, source_target_pairs={{7,0},{0,1},{1,2},{2,3},{3,4},{4,5},{5,6},{6,7},{15,8},{8,9},{9,10... | collective-permute-start | bytes 1572872 | tf_op jit(solution)/shard_map/ppermute | solution.py:10
  106.4 16.3 %collective-permute-start.4 = (bf16[32,8192]{1,0:T(8,128)(2,1)}, bf16[32,8192]{1,0:T(8,128)(2,1)S(1)}, u32[]{:S(2)}, u32[]{:S(2)}) collective-permute-start(bf16[32,8192]{1,0:T(8,128)(2,1)} %constant_dynamic-update-slice_fusion.4), channel_id=1, source_target_pairs={{1,0},{2,1},{3,2},{4,3},{5,4},{6,5},{7,6},{0,7},{9,8},{10,9},{11,1... | collective-permute-start | bytes 1572872 | tf_op jit(solution)/shard_map/ppermute | solution.py:10
  111.1 123.4 %reduce-scatter.9.cloned.1.call-start = ((), (), s32[]{:S(2)}) async-start(), calls=%async_computation.8 | async-start | bytes 1310720
  139.9 5.5 %collective-permute-start.5 = (bf16[32,2048]{1,0:T(8,128)(2,1)S(1)}, bf16[32,2048]{1,0:T(8,128)(2,1)S(1)}, u32[]{:S(2)}, u32[]{:S(2)}) collective-permute-start(bf16[32,2048]{1,0:T(8,128)(2,1)S(1)} %get-tuple-element.13), channel_id=1, source_target_pairs={{0,8},{8,16},{16,24},{24,0},{1,9},{9,17},{17,25},{25,1},{2,10},{10... | collective-permute-start | bytes 393224 | tf_op jit(solution)/shard_map/ppermute | solution.py:45
  145.4 35.6 %collective-permute-start.6 = (bf16[32,2048]{1,0:T(8,128)(2,1)S(1)}, bf16[32,2048]{1,0:T(8,128)(2,1)}, u32[]{:S(2)}, u32[]{:S(2)}) collective-permute-start(bf16[32,2048]{1,0:T(8,128)(2,1)S(1)} %collective-permute-done.5), channel_id=1, source_target_pairs={{0,8},{8,16},{16,24},{24,0},{1,9},{9,17},{17,25},{25,1},{2,10},{10... | collective-permute-start | bytes 393224 | tf_op jit(solution)/shard_map/ppermute | solution.py:45
  178.2 19.7 %collective-permute-start.13 = (f32[32,4,2048]{2,1,0:T(4,128)S(1)}, f32[32,4,2048]{2,1,0:T(4,128)S(1)}, u32[]{:S(2)}, u32[]{:S(2)}) collective-permute-start(f32[32,4,2048]{2,1,0:T(4,128)S(1)} %get-tuple-element.19), channel_id=1, source_target_pairs={{7,0},{0,1},{1,2},{2,3},{3,4},{4,5},{5,6},{6,7},{15,8},{8,9},{9,10... | collective-permute-start | bytes 3145736 | tf_op jit(solution)/shard_map/ppermute | solution.py:10
  179.7 13.9 %collective-permute-start.12 = (bf16[32,4,2048]{2,1,0:T(4,128)(2,1)S(1)}, bf16[32,4,2048]{2,1,0:T(4,128)(2,1)S(1)}, u32[]{:S(2)}, u32[]{:S(2)}) collective-permute-start(bf16[32,4,2048]{2,1,0:T(4,128)(2,1)S(1)} %fusion.18), channel_id=1, source_target_pairs={{1,0},{2,1},{3,2},{4,3},{5,4},{6,5},{7,6},{0,7},{9,8},{10,9},{11,1... | collective-permute-start | bytes 1572872 | tf_op jit(solution)/shard_map/ppermute | solution.py:10
  181.0 5.2 %collective-permute-start.7 = (bf16[32,2048]{1,0:T(8,128)(2,1)}, bf16[32,2048]{1,0:T(8,128)(2,1)S(1)}, u32[]{:S(2)}, u32[]{:S(2)}) collective-permute-start(bf16[32,2048]{1,0:T(8,128)(2,1)} %collective-permute-done.6), channel_id=1, source_target_pairs={{0,8},{8,16},{16,24},{24,0},{1,9},{9,17},{17,25},{25,1},{2,10},{10... | collective-permute-start | bytes 393224 | tf_op jit(solution)/shard_map/ppermute | solution.py:45
  186.9 21.3 %collective-permute-start.8 = (bf16[32,8192]{1,0:T(8,128)(2,1)}, bf16[32,8192]{1,0:T(8,128)(2,1)S(1)}, u32[]{:S(2)}, u32[]{:S(2)}) collective-permute-start(bf16[32,8192]{1,0:T(8,128)(2,1)} %constant_dynamic-update-slice_fusion), channel_id=1, source_target_pairs={{7,0},{0,1},{1,2},{2,3},{3,4},{4,5},{5,6},{6,7},{15,8},{8,9},{9,10... | collective-permute-start | bytes 1572872 | tf_op jit(solution)/shard_map/ppermute | solution.py:10
  189.1 19.1 %collective-permute-start.9 = (bf16[32,8192]{1,0:T(8,128)(2,1)}, bf16[32,8192]{1,0:T(8,128)(2,1)S(1)}, u32[]{:S(2)}, u32[]{:S(2)}) collective-permute-start(bf16[32,8192]{1,0:T(8,128)(2,1)} %constant_dynamic-update-slice_fusion), channel_id=1, source_target_pairs={{1,0},{2,1},{3,2},{4,3},{5,4},{6,5},{7,6},{0,7},{9,8},{10,9},{11,1... | collective-permute-start | bytes 1572872 | tf_op jit(solution)/shard_map/ppermute | solution.py:10
  245.9 49.8 %copy-start.3 = (f32[8,4,2048]{2,0,1:T(8,128)S(1)}, f32[8,4,2048]{2,0,1:T(8,128)}, u32[]{:S(2)}) copy-start(f32[8,4,2048]{2,0,1:T(8,128)} %copy-done) | copy-start | bytes 786436
  245.9 50.8 %all-to-all-start.4 = ((f32[32,32,192]{2,0,1:T(8,128)}), f32[32,32,192]{2,0,1:T(8,128)S(1)}, u32[]{:S(2)}, u32[]{:S(2)}) async-start(f32[32,32,192]{2,0,1:T(8,128)} %copy.91), calls=%async_computation.4 | async-start | bytes 2097152 | tf_op jit(solution)/shard_map/all_to_all | solution.py:110
  (14 other events, 235.5 us)
Sparse Core Ops, SparseCore 0:
  111.2 30.4 reduce-scatter.6
  200.1 34.3 reduce-scatter.8
